TPU v7x, 128 devices: a whole 4x4x4 slice. The times are simulated.
128 devices in a mesh: lat: 16 (over x, z_lo, core), lon: 8 (over z_hi, y).
Axes of the slice: x: 4, y: 4, z: 4 (z_hi: 2, z_lo: 2; z = z_hi * 2 + z_lo), core: 2. Of those that a mesh axis runs over, the one named last changes fastest.
Arguments:
- x_tiles: bfloat16 [8, 64, 77, 256], P('lon', 'lat'), may hold values from -6 to 6
- tile_pos: int32 [8, 64], P('lon', 'lat'), may hold values from 0 to 511, as said below
- valid_rows: int32 [8, 64], P('lon', 'lat'), may hold values from 1 to 16
- stem_w: bfloat16 [77, 200], replicated, may hold values from -0.625 to 0.625
- dw_kernel: float32 [200, 49], replicated, may hold values from -0.875 to 0.875
- norm_gain: float32 [200], replicated, may hold values from 0.1 to 1.9
- w_in: bfloat16 [200, 800], replicated, may hold values from -0.4375 to 0.4375
- w_out: bfloat16 [800, 200], replicated, may hold values from -0.21875 to 0.21875
- cotangent: bfloat16 [8, 64, 200, 256], P('lon', 'lat'), may hold values from -3072 to 3072
Outputs:
- out_tiles: bfloat16 [8, 64, 200, 256], P('lon', 'lat')
- grad_w_in: float32 [200, 800], replicated
- grad_w_out: float32 [800, 200], replicated
- grad_kernel: float32 [200, 49], replicated
- grad_gain: float32 [200], replicated
Inputs may be any that keep to these rules, and one draw needn't show every extreme that they name: `tile_pos`: in each sector the places are distinct; in the order of place, the r-th active tile of a sector is held by lat index r % 16. At most 2 tiles of one device lie in one band block of 32 tiles, and this is reached; some band block is fully active in every sector.
All inputs are finite; a program needn't handle non-finite values.
Results may differ from a plain program's by a relative error of at most 0.0075.
Values may be sent and summed in bfloat16 or wider, within the bound.
No kernel may reach another device: no remote copies, remote signals or barrier semaphores. Data moves between devices by JAX's collectives and lax.ppermute only.
A program may use at most 128 MiB of HBM per device.

v0:
```python
import jax
import jax.numpy as jnp
from jax import lax
from jax.sharding import PartitionSpec as P

C = 200
CIN = 77
KW = 7
TS = 16
BH = 64
BW = 128
K_TILES = 32


def extended(block, sides, width, periodic):
    for axis, dim in sides:
        count = lax.axis_size(axis)
        forward = [(i, i + 1) for i in range(count - 1)]
        if periodic:
            forward.append((count - 1, 0))
        backward = [(target, source) for source, target in forward]
        low = lax.ppermute(
            lax.slice_in_dim(block, block.shape[dim] - width, None, axis=dim), axis, forward
        )
        high = lax.ppermute(lax.slice_in_dim(block, 0, width, axis=dim), axis, backward)
        block = jnp.concatenate([low, block, high], axis=dim)
    return block


def gelu_tanh(value):
    return jax.nn.gelu(value, approximate=True)


def tiles_to_block(tiles):
    chan = tiles.shape[1]
    shaped = tiles.reshape(BH // TS, BW // TS, chan, TS, TS)
    return shaped.transpose(2, 0, 3, 1, 4).reshape(chan, BH, BW)


def block_to_tiles(block):
    chan = block.shape[0]
    shaped = block.reshape(chan, BH // TS, TS, BW // TS, TS)
    return shaped.transpose(1, 3, 0, 2, 4).reshape(K_TILES, chan, TS * TS)


def select_rows(onehot, tiles):
    return jnp.einsum("qa,acp->qcp", onehot, tiles, preferred_element_type=jnp.float32).astype(
        jnp.bfloat16
    )


def body(x_tiles, tile_pos, valid_rows, stem_w, dw_kernel, norm_gain, w_in, w_out, cotangent):
    f32 = jnp.float32
    bf16 = jnp.bfloat16
    lat_count = lax.axis_size("lat")
    per_pair = (K_TILES + lat_count - 1) // lat_count
    slot_count = lat_count * per_pair
    cells = TS * TS
    inputs = x_tiles[0]
    places = tile_pos[0]
    ocean_rows = valid_rows[0]
    upstream = cotangent[0]
    tile_count = inputs.shape[0]
    cell_rows = jnp.arange(cells, dtype=jnp.int32) // TS
    ocean = cell_rows[None, :] < ocean_rows[:, None]
    masked_in = jnp.where(ocean[:, None, :], inputs, jnp.zeros_like(inputs))
    stem_tiles = jnp.einsum("kc,akp->acp", stem_w, masked_in, preferred_element_type=f32).astype(
        bf16
    )
    band_of = places // K_TILES
    local_place = places - band_of * K_TILES
    tile_order = jnp.arange(tile_count, dtype=jnp.int32)
    earlier = (band_of[None, :] == band_of[:, None]) & (tile_order[None, :] < tile_order[:, None])
    rank_in = jnp.sum(earlier.astype(jnp.int32), axis=1)
    slot_of = band_of * per_pair + rank_in
    route_map = jnp.arange(slot_count, dtype=jnp.int32)[:, None] == slot_of[None, :]
    route_b = route_map.astype(bf16)
    slot_place = jnp.sum(jnp.where(route_map, local_place[None, :] + 1, 0), axis=1) - 1
    slot_place = slot_place.reshape(lat_count, per_pair)
    outgoing = select_rows(route_b, masked_in).reshape(lat_count, per_pair, CIN, cells)
    arrived_raw, arrived_place = (
        lax.all_to_all(outgoing, "lat", split_axis=0, concat_axis=0, tiled=True),
        lax.all_to_all(slot_place, "lat", split_axis=0, concat_axis=0, tiled=True),
    )
    arrived_raw = arrived_raw.reshape(slot_count, CIN, cells)
    arrived = jnp.einsum("kc,akp->acp", stem_w, arrived_raw, preferred_element_type=f32).astype(
        bf16
    )
    placing = (
        jnp.arange(K_TILES, dtype=jnp.int32)[:, None] == arrived_place.reshape(slot_count)[None, :]
    )
    placing_b = placing.astype(bf16)
    band_field = tiles_to_block(select_rows(placing_b, arrived))
    reach = KW // 2
    widened = extended(band_field, (("lon", 2),), reach, True)
    padded = extended(widened, (("lat", 1),), reach, False)

    def window(tap_index):
        row_off = tap_index // KW
        col_off = tap_index % KW
        return padded[:, row_off : row_off + BH, col_off : col_off + BW].astype(f32)

    conv_out = jnp.zeros(band_field.shape, f32)
    for tap_index in range(KW * KW):
        conv_out = conv_out + dw_kernel[:, tap_index][:, None, None] * window(tap_index)
    centred = conv_out - jnp.mean(conv_out, axis=0, keepdims=True)
    inv_std = lax.rsqrt(jnp.mean(centred * centred, axis=0, keepdims=True) + 1e-06)
    unit = centred * inv_std
    normed = (unit * norm_gain[:, None, None]).astype(bf16)
    returning = select_rows(placing_b.T, block_to_tiles(normed)).reshape(
        lat_count, per_pair, C, cells
    )
    returned = lax.all_to_all(returning, "lat", split_axis=0, concat_axis=0, tiled=True).reshape(
        slot_count, C, cells
    )
    features = select_rows(route_b.T, returned)
    preact = jnp.einsum("ch,acp->ahp", w_in, features, preferred_element_type=f32)
    hidden = gelu_tanh(preact).astype(bf16)
    branch = jnp.einsum("hc,ahp->acp", w_out, hidden, preferred_element_type=f32)
    result = jnp.where(ocean[:, None, :], stem_tiles.astype(f32) + branch, 0.0).astype(bf16)
    masked_grad = jnp.where(ocean[:, None, :], upstream, jnp.zeros_like(upstream))
    grad_hidden = jnp.einsum("hc,acp->ahp", w_out, masked_grad, preferred_element_type=f32)
    grad_preact = jax.vjp(gelu_tanh, preact)[1](grad_hidden)[0].astype(bf16)
    grad_feats = jnp.einsum("ch,ahp->acp", w_in, grad_preact, preferred_element_type=f32).astype(
        bf16
    )
    grad_outgoing = select_rows(route_b, grad_feats).reshape(lat_count, per_pair, C, cells)
    grad_arrived = lax.all_to_all(
        grad_outgoing, "lat", split_axis=0, concat_axis=0, tiled=True
    ).reshape(slot_count, C, cells)
    sum_in = jnp.einsum("acp,ahp->ch", features, grad_preact, preferred_element_type=f32)
    sum_out = jnp.einsum("ahp,acp->hc", hidden, masked_grad, preferred_element_type=f32)
    grad_field = tiles_to_block(select_rows(placing_b, grad_arrived)).astype(f32)
    scaled = grad_field * norm_gain[:, None, None]
    grad_conv = inv_std * (
        scaled
        - jnp.mean(scaled, axis=0, keepdims=True)
        - unit * jnp.mean(scaled * unit, axis=0, keepdims=True)
    )
    kernel_terms = []
    for tap_index in range(KW * KW):
        kernel_terms.append(jnp.sum(grad_conv * window(tap_index), axis=(1, 2)))
    sum_kernel = jnp.stack(kernel_terms, axis=1)
    sum_gain = jnp.sum(grad_field * unit, axis=(1, 2))
    cell_sum = TS * jnp.sum(ocean_rows.astype(f32))
    total_in, total_out, total_kernel, total_gain, cell_total = lax.psum(
        (sum_in, sum_out, sum_kernel, sum_gain, cell_sum), ("lat", "lon")
    )
    return (
        result[None],
        total_in / cell_total,
        total_out / cell_total,
        total_kernel / cell_total,
        total_gain / cell_total,
    )


def solution(mesh):
    in_specs = (
        P("lon", "lat", None, None),
        P("lon", "lat"),
        P("lon", "lat"),
        P(),
        P(),
        P(),
        P(),
        P(),
        P("lon", "lat", None, None),
    )
    out_specs = (P("lon", "lat", None, None), P(), P(), P(), P())
    return jax.shard_map(body, mesh=mesh, in_specs=in_specs, out_specs=out_specs, check_vma=False)
```

profile of v0, /device:TPU:2, one launch (start us, length us, event | category | flops | bytes accessed | tf_op | source)
XLA Modules:
  0.0 583.2 jit_solution(11858804636175604378)
XLA Ops:
  9.6 6.2 %all-to-all-start = ((s32[16,1,2]{2,1,0:T(1,128)}), s32[16,1,2]{2,1,0:T(1,128)S(1)}, u32[]{:S(2)}, u32[]{:S(2)}) async-start(s32[16,1,2]{2,1,0:T(1,128)} %bitcast.9), calls=%async_computation | async-start | bytes 16384 | tf_op jit(solution)/shard_map/all_to_all | solution.py:83
  20.5 5.7 all-to-all-start.1
  27.6 15.3 %all-to-all-done.1 = bf16[16,2,77,256]{3,1,2,0:T(2,128)(2,1)S(1)} async-done(((bf16[16,2,77,256]{3,1,2,0:T(2,128)(2,1)}), bf16[16,2,77,256]{3,1,2,0:T(2,128)(2,1)S(1)}, u32[]{:S(2)}, u32[]{:S(2)}) %all-to-all-start.1) | async-done | bytes 1261600 | tf_op jit(solution)/shard_map/all_to_all | solution.py:82
  46.9 7.2 %copy.72 = bf16[32,200,256]{1,2,0:T(8,128)(2,1)} copy(bf16[32,200,256]{2,0,1:T(8,128)(2,1)} %fusion.114) | data formatting | bytes 6553600 | tf_op jit(solution)/shard_map/convert_element_type | solution.py:47
  58.7 4.5 collective-permute-start.1
  68.4 4.7 collective-permute-start.3
  76.2 8.1 %maximum_maximum_fusion = (bf16[200,67,134]{0,2,1:T(8,128)(2,1)S(1)}, bf16[200,67,134]{0,2,1:T(8,128)(2,1)S(1)}) fusion(bf16[200,64,3]{0,2,1:T(4,128)(2,1)S(1)} %collective-permute-done.1, bf16[200,64,128]{0,2,1:T(8,128)(2,1)S(1)} %bitcast.228, bf16[200,64,3]{0,2,1:T(4,128)(2,1)S(1)} %collective-permute-done, ...), kind=kLoop, calls=%fused_computation.208 | loop fusion | flops 28729600 | bytes 10934400 | tf_op jit(solution)/shard_map/concatenate | solution.py:26
  84.3 68.1 %fusion.152 = (f32[64,128]{1,0:T(8,128)S(1)}, f32[200,64,128]{0,2,1:T(8,128)S(1)}) fusion(bf16[200,67,134]{0,2,1:T(8,128)(2,1)S(1)} %get-tuple-element.77, f32[200]{0:T(256)S(1)} %bitcast.286, f32[200]{0:T(256)S(1)} %bitcast.287, f32[200]{0:T(256)S(1)} %bitcast.240, f32[200]{0:T(256)S(1)} %bitcast.241, f32[200]{0:T(256)S(1)} %bitcast.242, ...), kind=kLoop, calls=%fused_computation.307 | loop fusion | flops 270327808 | bytes 147681568 | tf_op jit(solution)/shard_map/reduce_sum | solution.py:106
  160.2 7.3 %copy.76 = bf16[32,200,256]{2,0,1:T(8,128)(2,1)} copy(bf16[32,200,256]{1,2,0:T(8,128)(2,1)} %bitcast.237) | data formatting | bytes 6553600 | tf_op jit(solution)/shard_map/reshape | solution.py:43
  167.4 4.8 convolution_convert_fusion.1
  172.2 7.5 %reshape.217 = bf16[16,2,200,256]{3,1,0,2:T(2,128)(2,1)} reshape(bf16[32,200,256]{2,0,1:T(8,128)(2,1)} %convolution_convert_fusion.1) | data formatting | bytes 6553600 | tf_op jit(solution)/shard_map/reshape | solution.py:110
  179.8 4.2 copy.77
  183.9 45.5 %all_to_all.21 = bf16[16,2,200,256]{3,1,2,0:T(2,128)(2,1)S(1)} all-to-all(bf16[16,2,200,256]{3,1,2,0:T(2,128)(2,1)S(1)} %copy.77), channel_id=1, replica_groups=mesh['lat'=16,'lon'=8] {'lat'}, dimensions={0} | all-to-all | bytes 6553600 | tf_op jit(solution)/shard_map/all_to_all | solution.py:113
  229.4 5.5 copy.78
  234.9 7.8 %reshape.218 = bf16[32,200,256]{2,0,1:T(8,128)(2,1)} reshape(bf16[16,2,200,256]{3,1,0,2:T(2,128)(2,1)} %copy.78) | data formatting | bytes 6553600 | tf_op jit(solution)/shard_map/reshape | solution.py:113
  253.1 7.6 %reshape.219 = bf16[16,2,200,256]{3,1,0,2:T(2,128)(2,1)} reshape(bf16[32,200,256]{2,0,1:T(8,128)(2,1)} %convolution_convert_fusion) | data formatting | bytes 6553600 | tf_op jit(solution)/shard_map/reshape | solution.py:127
  260.7 5.8 %copy.82 = bf16[16,2,200,256]{3,1,2,0:T(2,128)(2,1)} copy(bf16[16,2,200,256]{3,1,0,2:T(2,128)(2,1)} %reshape.219) | data formatting | bytes 6553600 | tf_op jit(solution)/shard_map/reshape | solution.py:127
  266.5 6.0 %all-to-all-start.3 = ((bf16[16,2,200,256]{3,1,2,0:T(2,128)(2,1)}), bf16[16,2,200,256]{3,1,2,0:T(2,128)(2,1)}, u32[]{:S(2)}, u32[]{:S(2)}) async-start(bf16[16,2,200,256]{3,1,2,0:T(2,128)(2,1)} %copy.82), calls=%async_computation.3 | async-start | bytes 6553600 | tf_op jit(solution)/shard_map/all_to_all | solution.py:128
  276.7 4.2 convolution_bitcast_fusion
  285.0 27.7 %all-to-all-done.3 = bf16[16,2,200,256]{3,1,2,0:T(2,128)(2,1)} async-done(((bf16[16,2,200,256]{3,1,2,0:T(2,128)(2,1)}), bf16[16,2,200,256]{3,1,2,0:T(2,128)(2,1)}, u32[]{:S(2)}, u32[]{:S(2)}) %all-to-all-start.3) | async-done | bytes 3276832 | tf_op jit(solution)/shard_map/all_to_all | solution.py:128
  312.7 7.5 %copy.83 = bf16[16,2,200,256]{3,1,0,2:T(2,128)(2,1)} copy(bf16[16,2,200,256]{3,1,2,0:T(2,128)(2,1)} %all-to-all-done.3) | data formatting | bytes 6553600 | tf_op jit(solution)/shard_map/all_to_all | solution.py:128
  320.1 7.8 %reshape.220 = bf16[32,200,256]{2,0,1:T(8,128)(2,1)} reshape(bf16[16,2,200,256]{3,1,0,2:T(2,128)(2,1)} %copy.83) | data formatting | bytes 6553600 | tf_op jit(solution)/shard_map/reshape | solution.py:130
  327.9 5.7 convert_convert_fusion
  333.6 9.3 %copy.84 = f32[32,200,256]{1,2,0:T(8,128)} copy(f32[32,200,256]{2,0,1:T(8,128)} %convert_convert_fusion) | data formatting | bytes 13107200 | tf_op jit(solution)/shard_map/convert_element_type | solution.py:133
  342.9 4.6 multiply_reduce_fusion.2
  347.7 4.4 copy.85
  352.1 8.8 %multiply_reduce_fusion = (f32[200]{0:T(256)S(1)}, f32[64,128]{1,0:T(8,128)S(1)}) fusion(f32[200,64,128]{0,2,1:T(8,128)S(1)} %bitcast.231, f32[200,64,128]{0,2,1:T(8,128)} %copy-done.4, f32[64,128]{1,0:T(8,128)S(1)} %add_rsqrt_fusion, f32[64,128]{1,0:T(8,128)S(1)} %broadcast_multiply_fusion.1, f32[200]{0:T(256)S(1)} %copy-done.12), kind=kLoop, calls=%fused_computation.195 | loop fusion | flops 11460408 | bytes 13207104 | tf_op jit(solution)/shard_map/reduce_sum | solution.py:144
  360.9 50.6 %fusion.96 = (f32[200]{0:T(256)S(1)}, f32[200]{0:T(256)S(1)}, f32[200]{0:T(256)S(1)}, f32[200]{0:T(256)S(1)}, f32[200]{0:T(256)S(1)}, /*index=5*/f32[200]{0:T(25...) fusion(bf16[200,67,134]{0,2,1:T(8,128)(2,1)} %copy-done.3, ...), kind=kLoop, calls=%fused_computation.194 | loop fusion | flops 99938800 | bytes 78789472 | tf_op jit(solution)/shard_map/reduce_sum | solution.py:142
  411.5 49.7 %fusion.45 = (f32[200]{0:T(256)S(1)}, f32[200]{0:T(256)S(1)}, f32[200]{0:T(256)S(1)}, f32[200]{0:T(256)S(1)}, f32[200]{0:T(256)S(1)}, /*index=5*/f32[200]{0:T(25...) fusion(f32[200,64,128]{0,2,1:T(8,128)} %get-tuple-element.71, ...), kind=kLoop, calls=%fused_computation.143 | loop fusion | flops 88470000 | bytes 65550400 | tf_op jit(solution)/shard_map/reduce_sum | solution.py:142
  461.3 27.5 %fusion.78 = (f32[200]{0:T(256)S(1)}, f32[200]{0:T(256)S(1)}, f32[200]{0:T(256)S(1)}, f32[200]{0:T(256)S(1)}, f32[200]{0:T(256)S(1)}, /*index=5*/f32[200]{0:T(25...) fusion(f32[200,64,128]{0,2,1:T(8,128)} %get-tuple-element.71, ...), kind=kLoop, calls=%fused_computation.176 | loop fusion | flops 78641200 | bytes 19822400 | tf_op jit(solution)/shard_map/reduce_sum | solution.py:142
  488.9 4.3 fusion.27
  493.4 74.8 %all-reduce = (f32[]{:T(128)}, f32[200,49]{0,1:T(8,128)S(1)}, f32[200]{0:T(256)S(1)}) all-reduce(f32[]{:T(128)S(6)} %mul_shard_map.3, f32[200,49]{0,1:T(8,128)S(1)} %stack.199, f32[200]{0:T(256)S(1)} %get-tuple-element.5), channel_id=1, replica_groups=mesh['lat'=16,'lon'=8] {'lat','lon'}, use_global_device_ids=true, to_apply=%region_6.7 | all-reduce | flops 10001 | bytes 80008 | tf_op jit(solution)/shard_map/psum | solution.py:146
  (93 shorter events, 59.1 us)
Async XLA Ops:
  7.2 238.1 %copy-start = (bf16[200,800]{1,0:T(8,128)(2,1)S(1)}, bf16[200,800]{1,0:T(8,128)(2,1)}, u32[]{:S(2)}) copy-start(bf16[200,800]{1,0:T(8,128)(2,1)} %param.15) | copy-start | bytes 960004
  7.2 19.1 %copy-start.11 = (f32[200,49]{0,1:T(8,128)S(1)}, f32[200,49]{0,1:T(8,128)}, u32[]{:S(2)}) copy-start(f32[200,49]{0,1:T(8,128)} %param.13) | copy-start | bytes 117604
  7.2 35.9 %copy-start.10 = (bf16[77,200]{1,0:T(8,128)(2,1)S(1)}, bf16[77,200]{1,0:T(8,128)(2,1)}, u32[]{:S(2)}) copy-start(bf16[77,200]{1,0:T(8,128)(2,1)} %param.12) | copy-start | bytes 92404
  9.6 11.0 %all-to-all-start = ((s32[16,1,2]{2,1,0:T(1,128)}), s32[16,1,2]{2,1,0:T(1,128)S(1)}, u32[]{:S(2)}, u32[]{:S(2)}) async-start(s32[16,1,2]{2,1,0:T(1,128)} %bitcast.9), calls=%async_computation | async-start | bytes 16384 | tf_op jit(solution)/shard_map/all_to_all | solution.py:83
  20.5 22.4 %all-to-all-start.1 = ((bf16[16,2,77,256]{3,1,2,0:T(2,128)(2,1)}), bf16[16,2,77,256]{3,1,2,0:T(2,128)(2,1)S(1)}, u32[]{:S(2)}, u32[]{:S(2)}) async-start(bf16[16,2,77,256]{3,1,2,0:T(2,128)(2,1)} %copy.69), calls=%async_computation.1 | async-start | bytes 2523136 | tf_op jit(solution)/shard_map/all_to_all | solution.py:82
  56.9 27.4 %copy-start.6 = (bf16[200,4,16,8,16]{0,4,3,2,1:T(8,128)(2,1)}, bf16[200,4,16,8,16]{0,4,3,2,1:T(8,128)(2,1)S(1)}, u32[]{:S(2)}) copy-start(bf16[200,4,16,8,16]{0,4,3,2,1:T(8,128)(2,1)S(1)} %copy.73) | copy-start | bytes 9830404
  57.0 9.3 %collective-permute-start = (bf16[200,64,3]{0,2,1:T(4,128)(2,1)S(1)}, bf16[200,64,3]{0,2,1:T(4,128)(2,1)S(1)}, u32[]{:S(2)}, u32[]{:S(2)}) collective-permute-start(bf16[200,64,3]{0,2,1:T(4,128)(2,1)S(1)} %get-tuple-element.80), channel_id=1, source_target_pairs={{0,1},{1,2},{2,3},{3,4},{4,5},{5,6},{6,7},{7,0},{8,9},{9,10},{10,1... | collective-permute-start | bytes 230408 | tf_op jit(solution)/shard_map/ppermute | solution.py:22
  58.7 7.6 %collective-permute-start.1 = (bf16[200,64,3]{0,2,1:T(4,128)(2,1)S(1)}, bf16[200,64,3]{0,2,1:T(4,128)(2,1)S(1)}, u32[]{:S(2)}, u32[]{:S(2)}) collective-permute-start(bf16[200,64,3]{0,2,1:T(4,128)(2,1)S(1)} %get-tuple-element.81), channel_id=1, source_target_pairs={{1,0},{2,1},{3,2},{4,3},{5,4},{6,5},{7,6},{0,7},{9,8},{10,9},{11,1... | collective-permute-start | bytes 230408 | tf_op jit(solution)/shard_map/ppermute | solution.py:25
  66.5 8.0 %collective-permute-start.2 = (bf16[200,3,134]{0,2,1:T(8,128)(2,1)S(1)}, bf16[200,3,134]{0,2,1:T(8,128)(2,1)S(1)}, u32[]{:S(2)}, u32[]{:S(2)}) collective-permute-start(bf16[200,3,134]{0,2,1:T(8,128)(2,1)S(1)} %get-tuple-element.78), channel_id=1, source_target_pairs={{0,8},{8,16},{16,24},{24,32},{32,40},{40,48},{48,56},{56,64},{64,7... | collective-permute-start | bytes 482408 | tf_op jit(solution)/shard_map/ppermute | solution.py:22
  68.4 7.8 %collective-permute-start.3 = (bf16[200,3,134]{0,2,1:T(8,128)(2,1)S(1)}, bf16[200,3,134]{0,2,1:T(8,128)(2,1)S(1)}, u32[]{:S(2)}, u32[]{:S(2)}) collective-permute-start(bf16[200,3,134]{0,2,1:T(8,128)(2,1)S(1)} %get-tuple-element.79), channel_id=1, source_target_pairs={{8,0},{16,8},{24,16},{32,24},{40,32},{48,40},{56,48},{64,56},{72,6... | collective-permute-start | bytes 482408 | tf_op jit(solution)/shard_map/ppermute | solution.py:25
  84.3 68.1 %copy-start.2 = (bf16[200,67,134]{0,2,1:T(8,128)(2,1)}, bf16[200,67,134]{0,2,1:T(8,128)(2,1)S(1)}, u32[]{:S(2)}) copy-start(bf16[200,67,134]{0,2,1:T(8,128)(2,1)S(1)} %get-tuple-element.76) | copy-start | bytes 10773604
  84.3 68.1 %copy-start.3 = (bf16[200,67,134]{0,2,1:T(8,128)(2,1)}, bf16[200,67,134]{0,2,1:T(8,128)(2,1)S(1)}, u32[]{:S(2)}) copy-start(bf16[200,67,134]{0,2,1:T(8,128)(2,1)S(1)} %get-tuple-element.77) | copy-start | bytes 10773604
  152.5 5.1 copy-start.4
  152.5 2.5 copy-start.12
  234.9 11.0 %copy-start.14 = (bf16[800,200]{0,1:T(8,128)(2,1)S(1)}, bf16[800,200]{0,1:T(8,128)(2,1)}, u32[]{:S(2)}) copy-start(bf16[800,200]{0,1:T(8,128)(2,1)} %param.16) | copy-start | bytes 960004
  246.0 3.7 copy-start.8
  253.1 19.4 %copy-start.13 = (s32[1,4]{1,0:T(1,128)S(1)}, s32[1,4]{1,0:T(1,128)}, u32[]{:S(2)}) copy-start(s32[1,4]{1,0:T(1,128)} %param.11) | copy-start | bytes 52
  266.5 46.1 %all-to-all-start.3 = ((bf16[16,2,200,256]{3,1,2,0:T(2,128)(2,1)}), bf16[16,2,200,256]{3,1,2,0:T(2,128)(2,1)}, u32[]{:S(2)}, u32[]{:S(2)}) async-start(bf16[16,2,200,256]{3,1,2,0:T(2,128)(2,1)} %copy.82), calls=%async_computation.3 | async-start | bytes 6553600 | tf_op jit(solution)/shard_map/all_to_all | solution.py:128
  272.5 295.6 %all-reduce.4.cloned.1.call-start = ((), (), s32[]{:S(2)}) async-start(), calls=%async_computation.4 | async-start | bytes 2867200 | tf_op jit(solution)/shard_map/psum | solution.py:146
  276.7 4.3 copy-start.9
  352.1 8.8 %copy-start.7 = (f32[200,4,16,8,16]{0,4,3,2,1:T(8,128)}, f32[200,4,16,8,16]{0,4,3,2,1:T(8,128)S(1)}, u32[]{:S(2)}) copy-start(f32[200,4,16,8,16]{0,4,3,2,1:T(8,128)S(1)} %copy.85) | copy-start | bytes 19660804
  360.9 127.9 %slice-start = ((s8[4665344]{0:T(1024)(128)(4,1)}), s8[471040]{0:T(1024)(128)(4,1)S(1)}, s32[]{:S(2)}) async-start(s8[4665344]{0:T(1024)(128)(4,1)} %bitcast.224), calls=%async_computation.5 | async-start | bytes 942080
  411.5 77.3 %slice-start.1 = ((s8[4665344]{0:T(1024)(128)(4,1)}), s8[4194304]{0:T(1024)(128)(4,1)S(1)}, s32[]{:S(2)}) async-start(s8[4665344]{0:T(1024)(128)(4,1)} %bitcast.224), calls=%async_computation.6 | async-start | bytes 8388608
  461.3 27.6 %copy-start.5 = (f32[200,64,128]{0,2,1:T(8,128)S(1)}, f32[200,64,128]{0,2,1:T(8,128)}, u32[]{:S(2)}) copy-start(f32[200,64,128]{0,2,1:T(8,128)} %get-tuple-element.71) | copy-start | bytes 19660804
  461.3 114.9 %copy-start.1 = (bf16[200,800]{1,0:T(8,128)(2,1)S(1)}, bf16[200,800]{1,0:T(8,128)(2,1)}, u32[]{:S(2)}) copy-start(bf16[200,800]{1,0:T(8,128)(2,1)} %param.15) | copy-start | bytes 960004
Sparse Core Ops, SparseCore 0:
  281.1 168.1 all-reduce.3
where the time goes:
time: 590 us; the launch traced here: 583 us
  other arithmetic  240 us (41%)
  blocking collectives  120 us (20%)
  local copies, waits for them, and re-layouts  91.8 us (16%)
  waiting for transfers between devices  49.2 us (8%)
  matrix products  36.2 us (6%)
  starting transfers between devices  30.8 us (5%)
  between operations  15.4 us (3%)
    reduce_sum x4, other arithmetic, body(): kernel_terms.append(jnp.sum(grad_conv * window(tap_index), axis=(1, 2)))  132 us
    psum x1, blocking collectives, body(): lax.psum((sum_in, sum_out, sum_kernel, sum_gain, cell_sum), ('lat', 'lon'))  74.8 us
    reduce_sum x1, other arithmetic, body(): centred = conv_out - jnp.mean(conv_out, axis=0, keepdims=True)  68.1 us
    all_to_all x1, blocking collectives, body(): lax.all_to_all(returning, 'lat', split_axis=0, concat_axis=0, tiled=True)  45.5 us
    all_to_all x1, waiting for transfers between devices, body(): lax.all_to_all(grad_outgoing, 'lat', split_axis=0, concat_axis=0, tiled=T...  27.7 us
    dot_general x6, matrix products, select_rows(): jnp.einsum('qa,acp->qcp', onehot, tiles, preferred_element_type=jnp.float32)  19.1 us
    all_to_all x1, waiting for transfers between devices, body(): lax.all_to_all(outgoing, 'lat', split_axis=0, concat_axis=0, tiled=True)  15.3 us
    convert_element_type x2, local copies, waits for them, and re-layouts, body(): tiles_to_block(select_rows(placing_b, grad_arrived)).astype(f32)  13.7 us
  transfers between devices with their start and end apart: 8, of which 5 were waited for; matrix products, arithmetic and copies ran while one was open for 34% of the time, Pallas kernels for 0%

commit v1 on v0

--- a/solution.py
+++ b/solution.py
@@ -144,7 +144,7 @@
     sum_gain = jnp.sum(grad_field * unit, axis=(1, 2))
     cell_sum = TS * jnp.sum(ocean_rows.astype(f32))
     total_in, total_out, total_kernel, total_gain, cell_total = lax.psum(
-        (sum_in, sum_out, sum_kernel, sum_gain, cell_sum), ("lat", "lon")
+        lax.psum((sum_in, sum_out, sum_kernel, sum_gain, cell_sum), "lon"), "lat"
     )
     return (
         result[None],

time: 590 us -> 674 us (1.14)
  the two profiles are of different devices: /device:TPU:2 before, /device:TPU:0 now
where the time goes in v1:
time: 674 us; the launch traced here: 667 us
  other arithmetic  240 us (36%)
  blocking collectives  141 us (21%)
  waiting for transfers between devices  120 us (18%)
  local copies, waits for them, and re-layouts  91.8 us (14%)
  matrix products  35.3 us (5%)
  starting transfers between devices  24.1 us (4%)
  between operations  15.5 us (2%)
    reduce_sum x4, other arithmetic, body(): kernel_terms.append(jnp.sum(grad_conv * window(tap_index), axis=(1, 2)))  132 us
    psum x1, waiting for transfers between devices, body(): lax.psum((sum_in, sum_out, sum_kernel, sum_gain, cell_sum), 'lon')  95.2 us
    reduce_sum x1, other arithmetic, body(): centred = conv_out - jnp.mean(conv_out, axis=0, keepdims=True)  68.1 us
    psum x1, blocking collectives, body(): lax.psum(lax.psum((sum_in, sum_out, sum_kernel, sum_gain, cell_sum), 'lon...  53 us
    all_to_all x1, blocking collectives, body(): lax.all_to_all(returning, 'lat', split_axis=0, concat_axis=0, tiled=True)  48.9 us
    psum x1, blocking collectives, body(): lax.psum((sum_in, sum_out, sum_kernel, sum_gain, cell_sum), 'lon')  39 us
    dot_general x6, matrix products, select_rows(): jnp.einsum('qa,acp->qcp', onehot, tiles, preferred_element_type=jnp.float32)  19.1 us
    all_to_all x1, waiting for transfers between devices, body(): lax.all_to_all(outgoing, 'lat', split_axis=0, concat_axis=0, tiled=True)  17.4 us
  transfers between devices with their start and end apart: 9, of which 5 were waited for; matrix products, arithmetic and copies ran while one was open for 30% of the time, Pallas kernels for 0%

profile of v1, /device:TPU:0, one launch (start us, length us, event | category | flops | bytes accessed | tf_op | source)
XLA Modules:
  0.0 666.9 jit_solution(17828282939719616431)
XLA Ops:
  9.6 5.9 all-to-all-start
  21.4 4.5 all-to-all-start.1
  27.3 17.4 %all-to-all-done.1 = bf16[16,2,77,256]{3,1,2,0:T(2,128)(2,1)S(1)} async-done(((bf16[16,2,77,256]{3,1,2,0:T(2,128)(2,1)}), bf16[16,2,77,256]{3,1,2,0:T(2,128)(2,1)S(1)}, u32[]{:S(2)}, u32[]{:S(2)}) %all-to-all-start.1) | async-done | bytes 1261600 | tf_op jit(solution)/shard_map/all_to_all | solution.py:82
  48.7 7.2 %copy.72 = bf16[32,200,256]{1,2,0:T(8,128)(2,1)} copy(bf16[32,200,256]{2,0,1:T(8,128)(2,1)} %fusion.114) | data formatting | bytes 6553600 | tf_op jit(solution)/shard_map/convert_element_type | solution.py:47
  60.5 4.5 collective-permute-start.1
  73.9 8.1 %maximum_maximum_fusion = (bf16[200,67,134]{0,2,1:T(8,128)(2,1)S(1)}, bf16[200,67,134]{0,2,1:T(8,128)(2,1)S(1)}) fusion(bf16[200,64,3]{0,2,1:T(4,128)(2,1)S(1)} %collective-permute-done.1, bf16[200,64,128]{0,2,1:T(8,128)(2,1)S(1)} %bitcast.228, bf16[200,64,3]{0,2,1:T(4,128)(2,1)S(1)} %collective-permute-done, ...), kind=kLoop, calls=%fused_computation.208 | loop fusion | flops 28729600 | bytes 10934400 | tf_op jit(solution)/shard_map/concatenate | solution.py:26
  82.0 68.1 %fusion.152 = (f32[64,128]{1,0:T(8,128)S(1)}, f32[200,64,128]{0,2,1:T(8,128)S(1)}) fusion(bf16[200,67,134]{0,2,1:T(8,128)(2,1)S(1)} %get-tuple-element.82, f32[200]{0:T(256)S(1)} %bitcast.286, f32[200]{0:T(256)S(1)} %bitcast.287, f32[200]{0:T(256)S(1)} %bitcast.240, f32[200]{0:T(256)S(1)} %bitcast.241, f32[200]{0:T(256)S(1)} %bitcast.242, ...), kind=kLoop, calls=%fused_computation.307 | loop fusion | flops 270327808 | bytes 147681568 | tf_op jit(solution)/shard_map/reduce_sum | solution.py:106
  157.9 7.3 %copy.76 = bf16[32,200,256]{2,0,1:T(8,128)(2,1)} copy(bf16[32,200,256]{1,2,0:T(8,128)(2,1)} %bitcast.237) | data formatting | bytes 6553600 | tf_op jit(solution)/shard_map/reshape | solution.py:43
  165.1 4.8 convolution_convert_fusion.1
  169.9 7.5 %reshape.217 = bf16[16,2,200,256]{3,1,0,2:T(2,128)(2,1)} reshape(bf16[32,200,256]{2,0,1:T(8,128)(2,1)} %convolution_convert_fusion.1) | data formatting | bytes 6553600 | tf_op jit(solution)/shard_map/reshape | solution.py:110
  177.5 4.2 copy.77
  181.6 48.9 %all_to_all.21 = bf16[16,2,200,256]{3,1,2,0:T(2,128)(2,1)S(1)} all-to-all(bf16[16,2,200,256]{3,1,2,0:T(2,128)(2,1)S(1)} %copy.77), channel_id=1, replica_groups=mesh['lat'=16,'lon'=8] {'lat'}, dimensions={0} | all-to-all | bytes 6553600 | tf_op jit(solution)/shard_map/all_to_all | solution.py:113
  230.6 5.5 copy.78
  236.1 7.8 %reshape.218 = bf16[32,200,256]{2,0,1:T(8,128)(2,1)} reshape(bf16[16,2,200,256]{3,1,0,2:T(2,128)(2,1)} %copy.78) | data formatting | bytes 6553600 | tf_op jit(solution)/shard_map/reshape | solution.py:113
  254.3 7.5 %reshape.219 = bf16[16,2,200,256]{3,1,0,2:T(2,128)(2,1)} reshape(bf16[32,200,256]{2,0,1:T(8,128)(2,1)} %convolution_convert_fusion) | data formatting | bytes 6553600 | tf_op jit(solution)/shard_map/reshape | solution.py:127
  261.8 5.8 copy.82
  267.7 4.7 all-to-all-start.3
  274.0 4.2 convolution_bitcast_fusion
  283.9 95.2 %all-reduce.9.cloned.1.call-done = (f32[200,800]{1,0:T(8,128)}, f32[800,200]{0,1:T(8,128)}) async-done(((f32[200,800]{1,0:T(8,128)}, f32[800,200]{0,1:T(8,128)}), (f32[200,800]{1,0:T(8,128)}, f32[800,200]{0,1:T(8,128)})) %all-reduce.9.cloned.1.call-update) | async-done | bytes 1280016 | tf_op jit(solution)/shard_map/psum | solution.py:147
  379.1 7.4 %copy.83 = bf16[16,2,200,256]{3,1,0,2:T(2,128)(2,1)} copy(bf16[16,2,200,256]{3,1,2,0:T(2,128)(2,1)} %all-to-all-done.3) | data formatting | bytes 6553600 | tf_op jit(solution)/shard_map/all_to_all | solution.py:128
  386.5 7.8 %reshape.220 = bf16[32,200,256]{2,0,1:T(8,128)(2,1)} reshape(bf16[16,2,200,256]{3,1,0,2:T(2,128)(2,1)} %copy.83) | data formatting | bytes 6553600 | tf_op jit(solution)/shard_map/reshape | solution.py:130
  394.3 5.7 convert_convert_fusion
  400.0 9.3 %copy.84 = f32[32,200,256]{1,2,0:T(8,128)} copy(f32[32,200,256]{2,0,1:T(8,128)} %convert_convert_fusion) | data formatting | bytes 13107200 | tf_op jit(solution)/shard_map/convert_element_type | solution.py:133
  409.3 4.6 multiply_reduce_fusion.2
  414.1 4.4 copy.85
  418.6 8.8 %multiply_reduce_fusion = (f32[200]{0:T(256)S(1)}, f32[64,128]{1,0:T(8,128)S(1)}) fusion(f32[200,64,128]{0,2,1:T(8,128)S(1)} %bitcast.231, f32[200,64,128]{0,2,1:T(8,128)} %copy-done.4, f32[64,128]{1,0:T(8,128)S(1)} %add_rsqrt_fusion, f32[64,128]{1,0:T(8,128)S(1)} %broadcast_multiply_fusion.1, f32[200]{0:T(256)S(1)} %copy-done.11), kind=kLoop, calls=%fused_computation.195 | loop fusion | flops 11460408 | bytes 13207104 | tf_op jit(solution)/shard_map/reduce_sum | solution.py:144
  427.4 50.6 %fusion.96 = (f32[200]{0:T(256)S(1)}, f32[200]{0:T(256)S(1)}, f32[200]{0:T(256)S(1)}, f32[200]{0:T(256)S(1)}, f32[200]{0:T(256)S(1)}, /*index=5*/f32[200]{0:T(25...) fusion(bf16[200,67,134]{0,2,1:T(8,128)(2,1)} %copy-done.3, ...), kind=kLoop, calls=%fused_computation.194 | loop fusion | flops 99938800 | bytes 78789472 | tf_op jit(solution)/shard_map/reduce_sum | solution.py:142
  478.0 49.7 %fusion.45 = (f32[200]{0:T(256)S(1)}, f32[200]{0:T(256)S(1)}, f32[200]{0:T(256)S(1)}, f32[200]{0:T(256)S(1)}, f32[200]{0:T(256)S(1)}, /*index=5*/f32[200]{0:T(25...) fusion(f32[200,64,128]{0,2,1:T(8,128)} %get-tuple-element.76, ...), kind=kLoop, calls=%fused_computation.143 | loop fusion | flops 88470000 | bytes 65550400 | tf_op jit(solution)/shard_map/reduce_sum | solution.py:142
  527.8 27.5 %fusion.78 = (f32[200]{0:T(256)S(1)}, f32[200]{0:T(256)S(1)}, f32[200]{0:T(256)S(1)}, f32[200]{0:T(256)S(1)}, f32[200]{0:T(256)S(1)}, /*index=5*/f32[200]{0:T(25...) fusion(f32[200,64,128]{0,2,1:T(8,128)} %get-tuple-element.76, ...), kind=kLoop, calls=%fused_computation.176 | loop fusion | flops 78641200 | bytes 19822400 | tf_op jit(solution)/shard_map/reduce_sum | solution.py:142
  555.4 4.3 fusion.27
  559.8 39.0 %all-reduce.2 = (f32[]{:T(128)}, f32[200,49]{0,1:T(8,128)S(1)}, f32[200]{0:T(256)S(1)}) all-reduce(f32[]{:T(128)S(6)} %mul_shard_map.3, f32[200,49]{0,1:T(8,128)S(1)} %stack.199, f32[200]{0:T(256)S(1)} %get-tuple-element.5), channel_id=1, replica_groups=mesh['lat'=16,'lon'=8] {'lon'}, use_global_device_ids=true, to_apply=%region_7.8 | all-reduce | flops 10001 | bytes 80008 | tf_op jit(solution)/shard_map/psum | solution.py:147
  598.8 53.0 %all-reduce = (f32[]{:T(128)}, f32[200,49]{0,1:T(8,128)S(1)}, f32[200]{0:T(256)S(1)}) all-reduce(f32[]{:T(128)} %get-tuple-element.71, f32[200,49]{0,1:T(8,128)S(1)} %get-tuple-element.72, f32[200]{0:T(256)S(1)} %get-tuple-element.73), channel_id=1, replica_groups=mesh['lat'=16,'lon'=8] {'lat'}, use_global_device_ids=true, to_apply=%region_8.9 | all-reduce | flops 10001 | bytes 80008 | tf_op jit(solution)/shard_map/psum | solution.py:146
  (95 shorter events, 60.1 us)
Async XLA Ops:
  7.2 239.3 %copy-start = (bf16[200,800]{1,0:T(8,128)(2,1)S(1)}, bf16[200,800]{1,0:T(8,128)(2,1)}, u32[]{:S(2)}) copy-start(bf16[200,800]{1,0:T(8,128)(2,1)} %param.15) | copy-start | bytes 960004
  7.2 18.8 %copy-start.10 = (f32[200,49]{0,1:T(8,128)S(1)}, f32[200,49]{0,1:T(8,128)}, u32[]{:S(2)}) copy-start(f32[200,49]{0,1:T(8,128)} %param.13) | copy-start | bytes 117604
  7.2 37.7 %copy-start.9 = (bf16[77,200]{1,0:T(8,128)(2,1)S(1)}, bf16[77,200]{1,0:T(8,128)(2,1)}, u32[]{:S(2)}) copy-start(bf16[77,200]{1,0:T(8,128)(2,1)} %param.12) | copy-start | bytes 92404
  9.6 11.9 %all-to-all-start = ((s32[16,1,2]{2,1,0:T(1,128)}), s32[16,1,2]{2,1,0:T(1,128)S(1)}, u32[]{:S(2)}, u32[]{:S(2)}) async-start(s32[16,1,2]{2,1,0:T(1,128)} %bitcast.9), calls=%async_computation | async-start | bytes 16384 | tf_op jit(solution)/shard_map/all_to_all | solution.py:83
  21.4 23.2 %all-to-all-start.1 = ((bf16[16,2,77,256]{3,1,2,0:T(2,128)(2,1)}), bf16[16,2,77,256]{3,1,2,0:T(2,128)(2,1)S(1)}, u32[]{:S(2)}, u32[]{:S(2)}) async-start(bf16[16,2,77,256]{3,1,2,0:T(2,128)(2,1)} %copy.69), calls=%async_computation.1 | async-start | bytes 2523136 | tf_op jit(solution)/shard_map/all_to_all | solution.py:82
  58.7 23.4 %copy-start.6 = (bf16[200,4,16,8,16]{0,4,3,2,1:T(8,128)(2,1)}, bf16[200,4,16,8,16]{0,4,3,2,1:T(8,128)(2,1)S(1)}, u32[]{:S(2)}) copy-start(bf16[200,4,16,8,16]{0,4,3,2,1:T(8,128)(2,1)S(1)} %copy.73) | copy-start | bytes 9830404
  58.8 9.3 %collective-permute-start = (bf16[200,64,3]{0,2,1:T(4,128)(2,1)S(1)}, bf16[200,64,3]{0,2,1:T(4,128)(2,1)S(1)}, u32[]{:S(2)}, u32[]{:S(2)}) collective-permute-start(bf16[200,64,3]{0,2,1:T(4,128)(2,1)S(1)} %get-tuple-element.85), channel_id=1, source_target_pairs={{0,1},{1,2},{2,3},{3,4},{4,5},{5,6},{6,7},{7,0},{8,9},{9,10},{10,1... | collective-permute-start | bytes 230408 | tf_op jit(solution)/shard_map/ppermute | solution.py:22
  60.5 7.7 %collective-permute-start.1 = (bf16[200,64,3]{0,2,1:T(4,128)(2,1)S(1)}, bf16[200,64,3]{0,2,1:T(4,128)(2,1)S(1)}, u32[]{:S(2)}, u32[]{:S(2)}) collective-permute-start(bf16[200,64,3]{0,2,1:T(4,128)(2,1)S(1)} %get-tuple-element.86), channel_id=1, source_target_pairs={{1,0},{2,1},{3,2},{4,3},{5,4},{6,5},{7,6},{0,7},{9,8},{10,9},{11,1... | collective-permute-start | bytes 230408 | tf_op jit(solution)/shard_map/ppermute | solution.py:25
  68.2 2.8 collective-permute-start.2
  69.5 4.4 collective-permute-start.3
  82.0 68.1 %copy-start.2 = (bf16[200,67,134]{0,2,1:T(8,128)(2,1)}, bf16[200,67,134]{0,2,1:T(8,128)(2,1)S(1)}, u32[]{:S(2)}) copy-start(bf16[200,67,134]{0,2,1:T(8,128)(2,1)S(1)} %get-tuple-element.81) | copy-start | bytes 10773604
  82.0 68.1 %copy-start.3 = (bf16[200,67,134]{0,2,1:T(8,128)(2,1)}, bf16[200,67,134]{0,2,1:T(8,128)(2,1)S(1)}, u32[]{:S(2)}) copy-start(bf16[200,67,134]{0,2,1:T(8,128)(2,1)S(1)} %get-tuple-element.82) | copy-start | bytes 10773604
  150.2 5.1 copy-start.4
  150.2 2.5 copy-start.11
  236.1 11.0 %copy-start.13 = (bf16[800,200]{0,1:T(8,128)(2,1)S(1)}, bf16[800,200]{0,1:T(8,128)(2,1)}, u32[]{:S(2)}) copy-start(bf16[800,200]{0,1:T(8,128)(2,1)} %param.16) | copy-start | bytes 960004
  247.1 3.7 copy-start.8
  267.7 111.4 %all-to-all-start.3 = ((bf16[16,2,200,256]{3,1,2,0:T(2,128)(2,1)}), bf16[16,2,200,256]{3,1,2,0:T(2,128)(2,1)}, u32[]{:S(2)}, u32[]{:S(2)}) async-start(bf16[16,2,200,256]{3,1,2,0:T(2,128)(2,1)} %copy.82), calls=%async_computation.3 | async-start | bytes 6553600 | tf_op jit(solution)/shard_map/all_to_all | solution.py:128
  272.4 5.9 copy-start.12
  272.4 106.7 %all-reduce.9.cloned.1.call-start = ((), (), s32[]{:S(2)}) async-start(), calls=%async_computation.5 | async-start | bytes 2867200 | tf_op jit(solution)/shard_map/psum | solution.py:147
  278.2 373.7 %all-reduce.7.cloned.1.call-start = ((), (), s32[]{:S(2)}) async-start(), calls=%async_computation.4 | async-start | bytes 2867200 | tf_op jit(solution)/shard_map/psum | solution.py:146
  418.6 8.8 %copy-start.7 = (f32[200,4,16,8,16]{0,4,3,2,1:T(8,128)}, f32[200,4,16,8,16]{0,4,3,2,1:T(8,128)S(1)}, u32[]{:S(2)}) copy-start(f32[200,4,16,8,16]{0,4,3,2,1:T(8,128)S(1)} %copy.85) | copy-start | bytes 19660804
  427.4 127.9 %slice-start = ((s8[4665344]{0:T(1024)(128)(4,1)}), s8[471040]{0:T(1024)(128)(4,1)S(1)}, s32[]{:S(2)}) async-start(s8[4665344]{0:T(1024)(128)(4,1)} %bitcast.224), calls=%async_computation.6 | async-start | bytes 942080
  478.0 77.3 %slice-start.1 = ((s8[4665344]{0:T(1024)(128)(4,1)}), s8[4194304]{0:T(1024)(128)(4,1)S(1)}, s32[]{:S(2)}) async-start(s8[4665344]{0:T(1024)(128)(4,1)} %bitcast.224), calls=%async_computation.7 | async-start | bytes 8388608
  527.8 27.6 %copy-start.5 = (f32[200,64,128]{0,2,1:T(8,128)S(1)}, f32[200,64,128]{0,2,1:T(8,128)}, u32[]{:S(2)}) copy-start(f32[200,64,128]{0,2,1:T(8,128)} %get-tuple-element.76) | copy-start | bytes 19660804
  527.8 132.1 %copy-start.1 = (bf16[200,800]{1,0:T(8,128)(2,1)S(1)}, bf16[200,800]{1,0:T(8,128)(2,1)}, u32[]{:S(2)}) copy-start(bf16[200,800]{1,0:T(8,128)(2,1)} %param.15) | copy-start | bytes 960004
Sparse Core Ops, SparseCore 0:
  278.3 100.6 all-reduce.8
  381.6 119.8 all-reduce.6
